TPU v7x, 32 devices: a whole 2x2x4 slice. The times are simulated.
32 devices in a mesh: section: 2 (over x), img: 4 (over z), ch: 4 (over y, core).
Axes of the slice: x: 2, y: 2, z: 4, core: 2. Of those that a mesh axis runs over, the one named last changes fastest.
Arguments:
- pixels: bfloat16 [8, 32, 28, 640], P('img', 'ch'), may hold values from -6 to 6
- first_gain: float32 [640], replicated, may hold values from 0.25 to 1.75
- first_shift: float32 [640], replicated, may hold values from -3 to 3
- first_kernel: bfloat16 [3, 3, 640, 640], P(None, None, 'img'), may hold values from -0.078125 to 0.078125
- projection: bfloat16 [640, 2560], P('img'), may hold values from -0.25 to 0.25
- second_gain: float32 [2560], replicated, may hold values from 0.25 to 1.75
- second_shift: float32 [2560], replicated, may hold values from -3 to 3
- second_kernel: bfloat16 [3, 3, 2560, 2560], P(None, None, ('img', 'ch')), may hold values from -0.0390625 to 0.0390625
Outputs:
- section_outputs: bfloat16 [2, 8, 16, 14, 2560], P('section', 'img', 'ch')
All inputs are finite; a program needn't handle non-finite values.
Results may differ from a plain program's by a relative error of at most 0.013.
Values may be sent and summed in bfloat16 or wider, within the bound.
No kernel may reach another device: no remote copies, remote signals or barrier semaphores. Data moves between devices by JAX's collectives and lax.ppermute only.
A program may use at most 128 MiB of HBM per device.

v0:
```python
import jax
import jax.numpy as jnp
from jax import lax
from jax.sharding import PartitionSpec as P

LAYOUT = ("NHWC", "HWIO", "NHWC")


def extended(cells, sides, width):
    for axis, dim in sides:
        count = lax.axis_size(axis)
        ends = count - 1
        head = lax.slice_in_dim(cells, 0, width, axis=dim)
        tail = lax.slice_in_dim(cells, cells.shape[dim] - width, cells.shape[dim], axis=dim)
        cells = jnp.concatenate(
            [
                lax.ppermute(tail, axis, [(i, (i + 1) % count) for i in range(ends)]),
                cells,
                lax.ppermute(head, axis, [((i + 1) % count, i) for i in range(ends)]),
            ],
            axis=dim,
        )
    return cells


def from_behind(array, axis, by):
    count = lax.axis_size(axis)
    pairs = [(i, i + by) for i in range(count) if 0 <= i + by < count]
    return lax.ppermute(array, axis, pairs)


def convolve(inputs, kernel, padding):
    return lax.conv_general_dilated(
        inputs,
        kernel,
        (1, 1),
        padding,
        dimension_numbers=LAYOUT,
        preferred_element_type=jnp.float32,
    )


def reduce_resolution(value_entries):
    count, height, breadth, depth = value_entries.shape
    blocks = value_entries.reshape(count, height // 2, 2, breadth // 2, 2, depth)
    return jnp.sum(blocks, axis=(2, 4)) * 0.25


def pick_group(value_entries, groups, shards, member):
    lead = value_entries.shape[:-1]
    per_block = value_entries.shape[-1] // (groups * shards)
    split = value_entries.reshape(lead + (groups, shards, per_block))
    chosen = lax.dynamic_slice_in_dim(split, member, 1, len(lead) + 1)
    return chosen.reshape(lead + (groups * per_block,))


def arrange_groups(value_entries, groups, shards):
    lead = value_entries.shape[:-1]
    per_block = value_entries.shape[-1] // (groups * shards)
    split = value_entries.reshape(lead + (groups, shards, per_block))
    swapped = jnp.swapaxes(split, len(lead), len(lead) + 1)
    return swapped.reshape(lead + (groups * shards * per_block,))


def body(
    pixels,
    first_gain,
    first_shift,
    first_kernel,
    projection,
    second_gain,
    second_shift,
    second_kernel,
):
    section_id = lax.axis_index("section")
    is_first = section_id == 0
    is_second = section_id == 1
    groups = lax.axis_size("img")
    shards = lax.axis_size("ch")
    member = lax.axis_index("ch")
    images, rows, columns, depth = pixels.shape
    out_rows = rows // 2
    out_cols = columns // 2
    wide = second_gain.shape[0]
    normalized_input = jax.nn.relu(pixels.astype(jnp.float32) * first_gain + first_shift).astype(
        jnp.bfloat16
    )
    padded = extended(normalized_input, (("ch", 1),), 1)
    initial_blank = jnp.zeros((images, rows, columns, depth), jnp.float32)
    piece = lax.all_gather(first_kernel, "img", axis=2, tiled=True)

    def first_compute():
        return initial_blank + convolve(padded, piece, ((0, 0), (1, 1)))

    convolved = lax.cond(is_first, first_compute, lambda: initial_blank)
    blended_result = convolved + pixels.astype(jnp.float32)
    averaged_pixels = reduce_resolution(blended_result).astype(jnp.bfloat16)
    all_rows = out_rows * shards
    flat_pooled = averaged_pixels.reshape(images * out_rows * out_cols, depth)

    def project_piece(total, piece):

        def project_compute():
            return jnp.dot(flat_pooled, piece, preferred_element_type=jnp.float32)

        return lax.cond(is_first, project_compute, lambda: total)

    proj_empty = jnp.zeros((flat_pooled.shape[0], wide), jnp.float32)
    summed_proj = project_piece(proj_empty, lax.all_gather(projection, "img", axis=0, tiled=True))
    own_rows = summed_proj.astype(jnp.bfloat16).reshape(images, out_rows, out_cols, wide)
    arrived = from_behind(own_rows, "section", 1)
    sorted_layout = arrange_groups(arrived, groups, shards)
    channel_in = lax.all_to_all(sorted_layout, "ch", split_axis=3, concat_axis=1, tiled=True)
    gain_part = pick_group(second_gain, groups, shards, member)
    shift_part = pick_group(second_shift, groups, shards, member)
    second_in = jax.nn.relu(channel_in.astype(jnp.float32) * gain_part + shift_part).astype(
        jnp.bfloat16
    )

    def second_piece(total, piece):

        def second_compute():
            return total + convolve(second_in, piece, ((1, 1), (1, 1)))

        return lax.cond(is_second, second_compute, lambda: total)

    second_empty = jnp.zeros((images, all_rows, out_cols, wide), jnp.float32)
    partial_value = second_piece(
        second_empty, lax.all_gather(second_kernel, "img", axis=2, tiled=True)
    )
    summed = lax.psum_scatter(
        partial_value.astype(jnp.bfloat16), "ch", scatter_dimension=1, tiled=True
    ).astype(jnp.float32)
    block = (summed + arrived.astype(jnp.float32)).astype(jnp.bfloat16)
    final = jnp.where(is_first, own_rows, block)
    return final[None]


def solution(mesh):
    placed = (
        P("img", "ch", None, None),
        P(),
        P(),
        P(None, None, "img", None),
        P("img", None),
        P(),
        P(),
        P(None, None, ("img", "ch"), None),
    )
    return jax.shard_map(
        body,
        mesh=mesh,
        in_specs=placed,
        out_specs=P("section", "img", "ch", None, None),
        check_vma=False,
    )
```

profile of v0, /device:TPU:0, one launch (start us, length us, event | category | flops | bytes accessed | tf_op | source)
XLA Modules:
  0.0 794.3 jit_solution(10480101129916246538)
XLA Ops:
  6.5 0.7 all-gather.4.cloned.1.call-update
  7.3 0.7 all-gather.6.cloned.1.call-update
  8.1 0.7 all-gather.8.cloned.1.call-update
  9.4 2.4 collective-permute-start
  11.9 1.3 collective-permute-start.1
  13.2 4.1 collective-permute-done.1
  17.2 0.7 pad_maximum_fusion
  17.9 126.7 %all-gather.4.cloned.1.call-done = bf16[3,3,640,640]{3,2,1,0:T(8,128)(2,1)} async-done(((bf16[3,3,160,640]{3,2,1,0:T(8,128)(2,1)}), bf16[3,3,640,640]{3,2,1,0:T(8,128)(2,1)}) %all-gather.4.cloned.1.call-update) | async-done | bytes 7372816 | tf_op jit(solution)/shard_map/all_gather | solution.py:90
  144.7 10.0 %conditional.3 = (f32[2,8,28,640]{3,1,2,0:T(8,128)S(1)}) conditional(s32[]{:T(128)} %convert_element_type.54, () %tuple.26, (bf16[2,10,28,640]{3,1,2,0:T(8,128)(2,1)S(1)}, bf16[3,3,640,640]{3,2,1,0:T(8,128)(2,1)}) %tuple.27), branch_computations={%region_0.1_spmd, %region_1.2_spmd} | conditional | flops 3778887680 | bytes 21739878 | solution.py:95
  145.9 7.9 convolution_select_fusion
  153.8 0.8 copy.76
  154.8 0.9 copy.81
  155.7 0.6 reduce_sum.9
  156.4 53.6 %all-gather.6.cloned.1.call-done = bf16[640,2560]{1,0:T(8,128)(2,1)} async-done(((bf16[160,2560]{1,0:T(8,128)(2,1)}), bf16[640,2560]{1,0:T(8,128)(2,1)}) %all-gather.6.cloned.1.call-update) | async-done | bytes 3276816 | tf_op jit(solution)/shard_map/all_gather | solution.py:109
  210.1 3.3 conditional.4
  210.1 2.6 convolution_convert_fusion
  213.4 1.5 collective-permute-start.2
  214.9 12.1 %collective-permute-done.2 = bf16[2,4,14,2560]{3,1,2,0:T(4,128)(2,1)S(1)} collective-permute-done((bf16[2,4,14,2560]{3,1,2,0:T(4,128)(2,1)S(1)}, bf16[2,4,14,2560]{3,1,2,0:T(4,128)(2,1)S(1)}, u32[]{:S(2)}, u32[]{:S(2)}) %collective-permute-start.2) | collective-permute-done | bytes 573472 | tf_op jit(solution)/shard_map/ppermute | solution.py:29
  227.0 1.0 reshape.36
  228.0 5.6 copy.90
  233.7 10.3 %reshape.67 = bf16[4,2,35840]{2,1,0:T(2,128)(2,1)} reshape(bf16[2560,2,4,14]{3,2,1,0:T(4,128)(2,1)} %bitcast.54) | data formatting | bytes 1146880
  244.0 3.5 all-to-all-start
  247.9 8.9 %all-to-all-done = bf16[4,2,35840]{2,1,0:T(2,128)(2,1)S(1)} async-done(((bf16[4,2,35840]{2,1,0:T(2,128)(2,1)}), bf16[4,2,35840]{2,1,0:T(2,128)(2,1)S(1)}, u32[]{:S(2)}, u32[]{:S(2)}) %all-to-all-start) | async-done | bytes 573472 | tf_op jit(solution)/shard_map/all_to_all | solution.py:113
  256.8 12.7 %reshape.68 = bf16[2560,2,4,14]{3,2,1,0:T(4,128)(2,1)} reshape(bf16[4,2,35840]{2,1,0:T(2,128)(2,1)S(1)} %all-to-all-done) | data formatting | bytes 1146880
  269.5 6.8 copy.86
  276.7 0.9 copy.87
  277.6 0.8 fusion.27
  278.4 427.1 %all-gather.8.cloned.1.call-done = bf16[3,3,640,2560]{3,2,1,0:T(8,128)(2,1)} async-done(((bf16[3,3,160,2560]{3,2,1,0:T(8,128)(2,1)}), bf16[3,3,640,2560]{3,2,1,0:T(8,128)(2,1)}) %all-gather.8.cloned.1.call-update) | async-done | bytes 29491216 | tf_op jit(solution)/shard_map/all_gather | solution.py:129
  705.9 1.4 copy-done
  707.3 0.6 dynamic-slice
  708.6 76.5 %all-reduce.3.cloned.1.call-done = bf16[2,16,14,2560]{3,1,2,0:T(8,128)(2,1)} async-done(((bf16[2,16,14,2560]{3,1,2,0:T(8,128)(2,1)}), bf16[2,16,14,2560]{3,1,2,0:T(8,128)(2,1)}) %all-reduce.3.cloned.1.call-update) | async-done | bytes 2293776
  785.1 2.7 fusion.29
  (47 shorter events, 4.5 us)
Async XLA Ops:
  6.5 138.1 %all-gather.4.cloned.1.call-start = ((), (), s32[]{:S(2)}) async-start(), calls=%async_computation.1 | async-start | bytes 9216000 | tf_op jit(solution)/shard_map/all_gather | solution.py:90
  7.3 202.8 %all-gather.6.cloned.1.call-start = ((), (), s32[]{:S(2)}) async-start(), calls=%async_computation.2 | async-start | bytes 4096000 | tf_op jit(solution)/shard_map/all_gather | solution.py:109
  8.0 1.1 copy-start.1
  8.0 1.1 copy-start.6
  8.0 1.0 copy-start.7
  8.0 697.4 %all-gather.8.cloned.1.call-start = ((), (), s32[]{:S(2)}) async-start(), calls=%async_computation.3 | async-start | bytes 36864000 | tf_op jit(solution)/shard_map/all_gather | solution.py:129
  9.4 3.7 collective-permute-start
  11.9 5.4 collective-permute-start.1
  145.2 0.7 copy-start.9
  213.4 20.3 %copy-start.2 = (bf16[2,4,14,2560]{3,1,2,0:T(4,128)(2,1)}, bf16[2,4,14,2560]{3,1,2,0:T(4,128)(2,1)S(1)}, u32[]{:S(2)}) copy-start(bf16[2,4,14,2560]{3,1,2,0:T(4,128)(2,1)S(1)} %get-tuple-element.60) | copy-start | bytes 1720324
  213.4 13.6 %collective-permute-start.2 = (bf16[2,4,14,2560]{3,1,2,0:T(4,128)(2,1)S(1)}, bf16[2,4,14,2560]{3,1,2,0:T(4,128)(2,1)S(1)}, u32[]{:S(2)}, u32[]{:S(2)}) collective-permute-start(bf16[2,4,14,2560]{3,1,2,0:T(4,128)(2,1)S(1)} %get-tuple-element.60), channel_id=1, source_target_pairs={{0,16},{1,17},{2,18},{3,19},{4,20},{5,21},{6,22},{7,23},{8,24},{9,... | collective-permute-start | bytes 1720328 | tf_op jit(solution)/shard_map/ppermute | solution.py:29
  233.7 13.8 %copy-start.4 = (f32[2560]{0:T(1024)S(1)}, f32[2560]{0:T(1024)}, u32[]{:S(2)}) copy-start(f32[2560]{0:T(1024)} %param.19) | copy-start | bytes 30724
  233.7 13.9 %copy-start.5 = (f32[2560]{0:T(1024)S(1)}, f32[2560]{0:T(1024)}, u32[]{:S(2)}) copy-start(f32[2560]{0:T(1024)} %param.20) | copy-start | bytes 30724
  244.0 12.8 %all-to-all-start = ((bf16[4,2,35840]{2,1,0:T(2,128)(2,1)}), bf16[4,2,35840]{2,1,0:T(2,128)(2,1)S(1)}, u32[]{:S(2)}, u32[]{:S(2)}) async-start(bf16[4,2,35840]{2,1,0:T(2,128)(2,1)} %reshape.67), calls=%async_computation | async-start | bytes 1146880 | tf_op jit(solution)/shard_map/all_to_all | solution.py:113
  247.4 537.6 %all-reduce.3.cloned.1.call-start = ((), (), s32[]{:S(2)}) async-start(), calls=%async_computation.4 | async-start | bytes 4587520
  705.9 1.4 copy-start
  705.9 1.4 copy-start.8
  705.9 79.2 %copy-start.3 = (bf16[2,4,14,2560]{3,1,2,0:T(4,128)(2,1)S(1)}, bf16[2,4,14,2560]{3,1,2,0:T(4,128)(2,1)}, u32[]{:S(2)}) copy-start(bf16[2,4,14,2560]{3,1,2,0:T(4,128)(2,1)} %copy-done.2) | copy-start | bytes 1720324
Sparse Core Ops, SparseCore 0:
  8.9 135.7 all-gather.3
  146.2 63.7 all-gather.5
  211.6 493.7 all-gather.7
  707.7 77.3 all-reduce.2
where the time goes:
time: 795 us; the launch traced here: 794 us
  waiting for transfers between devices  711 us (89%)
  local copies, waits for them, and re-layouts  44.5 us (6%)
  between operations  14 us (2%)
  matrix products  10.5 us (1%)
  starting transfers between devices  8.8 us (1%)
    all_gather x1, waiting for transfers between devices, body(): lax.all_gather(second_kernel, 'img', axis=2, tiled=True)  427 us
    all_gather x1, waiting for transfers between devices, body(): piece = lax.all_gather(first_kernel, 'img', axis=2, tiled=True)  127 us
    unnamed x5, waiting for transfers between devices  78.6 us
    all_gather x1, waiting for transfers between devices, body(): lax.all_gather(projection, 'img', axis=0, tiled=True)  53.6 us
    unnamed x21, local copies, waits for them, and re-layouts  25.4 us
  transfers between devices with their start and end apart: 8, of which 7 were waited for; matrix products, arithmetic and copies ran while one was open for 7% of the time, Pallas kernels for 0%

commit v1 on v0

--- a/solution.py
+++ b/solution.py
@@ -87,7 +87,12 @@
     )
     padded = extended(normalized_input, (("ch", 1),), 1)
     initial_blank = jnp.zeros((images, rows, columns, depth), jnp.float32)
-    piece = lax.all_gather(first_kernel, "img", axis=2, tiled=True)
+    ring = [first_kernel]
+    for hop in range(3):
+        ring.append(lax.ppermute(ring[-1], "img", [(dev, (dev + 1) % 4) for dev in range(4)]))
+    piece = jnp.roll(
+        jnp.concatenate(ring[::-1], axis=2), (lax.axis_index("img") + 1) * ring[0].shape[2], axis=2
+    )
 
     def first_compute():
         return initial_blank + convolve(padded, piece, ((0, 0), (1, 1)))

time: 795 us -> 754 us (0.948)
  waiting for transfers between devices: 711 us -> 591 us
  starting transfers between devices: 8.8 us -> 65.5 us
  local copies, waits for them, and re-layouts: 44.5 us -> 64.1 us
    ppermute x0 -> x3, waiting for transfers between devices: none -> 203 us  [body(): lax.ppermute(ring[-1], 'img', [(dev, (dev + 1) % 4) for dev in range(4)])]
    all_gather x1, waiting for transfers between devices: 427 us -> 290 us  [body(): lax.all_gather(second_kernel, 'img', axis=2, tiled=True)]
    all_gather x1 -> x0, waiting for transfers between devices: 127 us -> none  [body(): piece = lax.all_gather(first_kernel, 'img', axis=2, tiled=True)]
    ppermute x0 -> x3, starting transfers between devices: none -> 58.1 us  [body(): lax.ppermute(ring[-1], 'img', [(dev, (dev + 1) % 4) for dev in range(4)])]
    all_gather x1, waiting for transfers between devices: 53.6 us -> 0.02 us  [body(): lax.all_gather(projection, 'img', axis=0, tiled=True)]
    unnamed x21 -> x36, local copies, waits for them, and re-layouts: 25.4 us -> 43.7 us
    unnamed x5 -> x4, waiting for transfers between devices: 78.6 us -> 78.9 us
  transfers between devices with their start and end apart: 8 -> 10, of which waited for: 7 -> 8; matrix products, arithmetic and copies ran while one was open for 7% -> 10% of each run, Pallas kernels for 0% -> 0%
where the time goes in v1:
time: 754 us; the launch traced here: 753 us
  waiting for transfers between devices  591 us (78%)
  starting transfers between devices  65.5 us (9%)
  local copies, waits for them, and re-layouts  64.1 us (9%)
  between operations  13.9 us (2%)
  matrix products  10.7 us (1%)
    all_gather x1, waiting for transfers between devices, body(): lax.all_gather(second_kernel, 'img', axis=2, tiled=True)  290 us
    ppermute x3, waiting for transfers between devices, body(): lax.ppermute(ring[-1], 'img', [(dev, (dev + 1) % 4) for dev in range(4)])  203 us
    unnamed x4, waiting for transfers between devices  78.9 us
    ppermute x3, starting transfers between devices, body(): lax.ppermute(ring[-1], 'img', [(dev, (dev + 1) % 4) for dev in range(4)])  58.1 us
    unnamed x36, local copies, waits for them, and re-layouts  43.7 us
  transfers between devices with their start and end apart: 10, of which 8 were waited for; matrix products, arithmetic and copies ran while one was open for 10% of the time, Pallas kernels for 0%

profile of v1, /device:TPU:0, one launch (start us, length us, event | category | flops | bytes accessed | tf_op | source)
XLA Modules:
  0.0 752.9 jit_solution(7250545830102872984)
XLA Ops:
  8.8 3.1 collective-permute-start
  11.8 72.9 %collective-permute-done = bf16[3,3,160,640]{3,2,1,0:T(8,128)(2,1)S(1)} collective-permute-done((bf16[3,3,160,640]{3,2,1,0:T(8,128)(2,1)S(1)}, bf16[3,3,160,640]{3,2,1,0:T(8,128)(2,1)S(1)}, u32[]{:S(2)}, u32[]{:S(2)}) %collective-permute-start) | collective-permute-done | bytes 1843232 | tf_op jit(solution)/shard_map/ppermute | solution.py:92
  86.0 20.8 %collective-permute-start.1 = (bf16[3,3,160,640]{3,2,1,0:T(8,128)(2,1)S(1)}, bf16[3,3,160,640]{3,2,1,0:T(8,128)(2,1)}, u32[]{:S(2)}, u32[]{:S(2)}) collective-permute-start(bf16[3,3,160,640]{3,2,1,0:T(8,128)(2,1)S(1)} %collective-permute-done), channel_id=1, source_target_pairs={{0,4},{4,8},{8,12},{12,0},{1,5},{5,9},{9,13},{13,1},{2,6},{6,10},{... | collective-permute-start | bytes 5529608 | tf_op jit(solution)/shard_map/ppermute | solution.py:92
  106.7 65.7 %collective-permute-done.1 = bf16[3,3,160,640]{3,2,1,0:T(8,128)(2,1)} collective-permute-done((bf16[3,3,160,640]{3,2,1,0:T(8,128)(2,1)S(1)}, bf16[3,3,160,640]{3,2,1,0:T(8,128)(2,1)}, u32[]{:S(2)}, u32[]{:S(2)}) %collective-permute-start.1) | collective-permute-done | bytes 1843232 | tf_op jit(solution)/shard_map/ppermute | solution.py:92
  172.4 34.2 %collective-permute-start.2 = (bf16[3,3,160,640]{3,2,1,0:T(8,128)(2,1)}, bf16[3,3,160,640]{3,2,1,0:T(8,128)(2,1)}, u32[]{:S(2)}, u32[]{:S(2)}) collective-permute-start(bf16[3,3,160,640]{3,2,1,0:T(8,128)(2,1)} %collective-permute-done.1), channel_id=1, source_target_pairs={{0,4},{4,8},{8,12},{12,0},{1,5},{5,9},{9,13},{13,1},{2,6},{6,10},{... | collective-permute-start | bytes 5529608 | tf_op jit(solution)/shard_map/ppermute | solution.py:92
  210.5 3.3 collective-permute-done.4
  213.8 1.8 pad_maximum_fusion
  215.5 64.4 %collective-permute-done.2 = bf16[3,3,160,640]{3,2,1,0:T(8,128)(2,1)} collective-permute-done((bf16[3,3,160,640]{3,2,1,0:T(8,128)(2,1)}, bf16[3,3,160,640]{3,2,1,0:T(8,128)(2,1)}, u32[]{:S(2)}, u32[]{:S(2)}) %collective-permute-start.2) | collective-permute-done | bytes 1843232 | tf_op jit(solution)/shard_map/ppermute | solution.py:92
  279.9 2.9 constant_dynamic-update-slice_fusion.7
  282.8 3.1 constant_dynamic-update-slice_fusion.6
  285.9 1.4 constant_dynamic-update-slice_fusion.5
  287.3 1.4 constant_dynamic-update-slice_fusion.4
  288.7 2.9 constant_dynamic-update-slice_fusion.3
  291.6 2.9 constant_dynamic-update-slice_fusion.2
  294.6 1.4 constant_dynamic-update-slice_fusion.1
  296.0 1.4 constant_dynamic-update-slice_fusion
  297.4 10.0 %conditional.3 = (f32[2,8,28,640]{3,1,2,0:T(8,128)S(1)}) conditional(s32[]{:T(128)} %convert_element_type.54, () %tuple.36, (s32[]{:T(128)}, bf16[3,3,1280,640]{3,2,1,0:T(8,128)(2,1)}, bf16[2,10,28,640]{3,1,2,0:T(8,128)(2,1)S(1)}) %tuple.37), branch_computations={%region_0.1_spmd, %region_1.2_spmd} | conditional | flops 3778887680 | bytes 21740010 | solution.py:100
  298.5 8.1 %fusion.3 = f32[8,16,4,640]{3,1,2,0:T(8,128)S(1)} fusion(bf16[3,3,1280,640]{3,2,1,0:T(8,128)(2,1)} %get-tuple-element.104, s32[]{:T(128)S(6)} %select_n.28, bf16[10,2,7,2,640]{4,2,1,3,0:T(8,128)(2,1)S(1)} %slice.12, bf16[10,2,8,4,640]{4,2,1,3,0:T(8,128)(2,1)S(1)} %copy.75, pred[16,4]{0,1:T(4,128)(4,1)S(1)} %copy-done.13), kind=kOutput, calls=%fused_computation.4 | convolution fusion | flops 3778887680 | bytes 9861188 | tf_op jit(solution)/shard_map/cond/branch_1_fun/conv_general_dilated | solution.py:33
  310.2 3.5 conditional.4
  310.5 2.6 convolution_convert_fusion
  313.8 1.3 collective-permute-start.5
  315.1 7.2 collective-permute-done.5
  323.3 5.7 copy.90
  329.0 10.2 %reshape.67 = bf16[4,2,35840]{2,1,0:T(2,128)(2,1)} reshape(bf16[2560,2,4,14]{3,2,1,0:T(4,128)(2,1)} %bitcast.53) | data formatting | bytes 1146880
  339.2 3.5 all-to-all-start
  343.1 8.9 %all-to-all-done = bf16[4,2,35840]{2,1,0:T(2,128)(2,1)S(1)} async-done(((bf16[4,2,35840]{2,1,0:T(2,128)(2,1)}), bf16[4,2,35840]{2,1,0:T(2,128)(2,1)S(1)}, u32[]{:S(2)}, u32[]{:S(2)}) %all-to-all-start) | async-done | bytes 573472 | tf_op jit(solution)/shard_map/all_to_all | solution.py:118
  352.0 12.7 %reshape.68 = bf16[2560,2,4,14]{3,2,1,0:T(4,128)(2,1)} reshape(bf16[4,2,35840]{2,1,0:T(2,128)(2,1)S(1)} %all-to-all-done) | data formatting | bytes 1146880
  364.7 6.8 copy.86
  373.6 289.7 %all-gather.5.cloned.1.call-done = bf16[3,3,640,2560]{3,2,1,0:T(8,128)(2,1)} async-done(((bf16[3,3,160,2560]{3,2,1,0:T(8,128)(2,1)}), bf16[3,3,640,2560]{3,2,1,0:T(8,128)(2,1)}) %all-gather.5.cloned.1.call-update) | async-done | bytes 29491216 | tf_op jit(solution)/shard_map/all_gather | solution.py:134
  663.8 1.4 copy-done
  666.3 77.5 %all-reduce.3.cloned.1.call-done = bf16[2,16,14,2560]{3,1,2,0:T(8,128)(2,1)} async-done(((bf16[2,16,14,2560]{3,1,2,0:T(8,128)(2,1)}), bf16[2,16,14,2560]{3,1,2,0:T(8,128)(2,1)}) %all-reduce.3.cloned.1.call-update) | async-done | bytes 2293776
  743.7 2.7 fusion.35
  (66 shorter events, 17.3 us)
Async XLA Ops:
  6.5 303.7 %all-gather.3.cloned.1.call-start = ((), (), s32[]{:S(2)}) async-start(), calls=%async_computation.1 | async-start | bytes 4096000 | tf_op jit(solution)/shard_map/all_gather | solution.py:114
  7.3 1.5 copy-start.1
  7.3 199.4 %copy-start.5 = (bf16[2,8,28,640]{3,1,2,0:T(8,128)(2,1)S(1)}, bf16[2,8,28,640]{3,1,2,0:T(8,128)(2,1)}, u32[]{:S(2)}) copy-start(bf16[2,8,28,640]{3,1,2,0:T(8,128)(2,1)} %param.14) | copy-start | bytes 1720324
  7.3 199.4 %copy-start.10 = (f32[640]{0:T(1024)S(1)}, f32[640]{0:T(1024)}, u32[]{:S(2)}) copy-start(f32[640]{0:T(1024)} %param.16) | copy-start | bytes 7684
  7.3 199.4 %copy-start.11 = (f32[640]{0:T(1024)S(1)}, f32[640]{0:T(1024)}, u32[]{:S(2)}) copy-start(f32[640]{0:T(1024)} %param.15) | copy-start | bytes 7684
  7.3 656.0 %all-gather.5.cloned.1.call-start = ((), (), s32[]{:S(2)}) async-start(), calls=%async_computation.2 | async-start | bytes 36864000 | tf_op jit(solution)/shard_map/all_gather | solution.py:134
  8.8 76.0 %collective-permute-start = (bf16[3,3,160,640]{3,2,1,0:T(8,128)(2,1)S(1)}, bf16[3,3,160,640]{3,2,1,0:T(8,128)(2,1)S(1)}, u32[]{:S(2)}, u32[]{:S(2)}) collective-permute-start(bf16[3,3,160,640]{3,2,1,0:T(8,128)(2,1)S(1)} %copy-done.1), channel_id=1, source_target_pairs={{0,4},{4,8},{8,12},{12,0},{1,5},{5,9},{9,13},{13,1},{2,6},{6,10},{... | collective-permute-start | bytes 5529608 | tf_op jit(solution)/shard_map/ppermute | solution.py:92
  84.7 1.2 copy-start.2
  86.0 86.5 %collective-permute-start.1 = (bf16[3,3,160,640]{3,2,1,0:T(8,128)(2,1)S(1)}, bf16[3,3,160,640]{3,2,1,0:T(8,128)(2,1)}, u32[]{:S(2)}, u32[]{:S(2)}) collective-permute-start(bf16[3,3,160,640]{3,2,1,0:T(8,128)(2,1)S(1)} %collective-permute-done), channel_id=1, source_target_pairs={{0,4},{4,8},{8,12},{12,0},{1,5},{5,9},{9,13},{13,1},{2,6},{6,10},{... | collective-permute-start | bytes 5529608 | tf_op jit(solution)/shard_map/ppermute | solution.py:92
  172.4 107.5 %collective-permute-start.2 = (bf16[3,3,160,640]{3,2,1,0:T(8,128)(2,1)}, bf16[3,3,160,640]{3,2,1,0:T(8,128)(2,1)}, u32[]{:S(2)}, u32[]{:S(2)}) collective-permute-start(bf16[3,3,160,640]{3,2,1,0:T(8,128)(2,1)} %collective-permute-done.1), channel_id=1, source_target_pairs={{0,4},{4,8},{8,12},{12,0},{1,5},{5,9},{9,13},{13,1},{2,6},{6,10},{... | collective-permute-start | bytes 5529608 | tf_op jit(solution)/shard_map/ppermute | solution.py:92
  206.8 0.8 copy-start.4
  207.8 2.6 collective-permute-start.3
  209.1 4.6 collective-permute-start.4
  282.8 3.1 copy-start.3
  297.8 0.7 copy-start.13
  313.8 15.2 %copy-start.6 = (bf16[2,4,14,2560]{3,1,2,0:T(4,128)(2,1)}, bf16[2,4,14,2560]{3,1,2,0:T(4,128)(2,1)S(1)}, u32[]{:S(2)}) copy-start(bf16[2,4,14,2560]{3,1,2,0:T(4,128)(2,1)S(1)} %get-tuple-element.143) | copy-start | bytes 1720324
  313.8 8.5 %collective-permute-start.5 = (bf16[2,4,14,2560]{3,1,2,0:T(4,128)(2,1)S(1)}, bf16[2,4,14,2560]{3,1,2,0:T(4,128)(2,1)S(1)}, u32[]{:S(2)}, u32[]{:S(2)}) collective-permute-start(bf16[2,4,14,2560]{3,1,2,0:T(4,128)(2,1)S(1)} %get-tuple-element.143), channel_id=1, source_target_pairs={{0,16},{1,17},{2,18},{3,19},{4,20},{5,21},{6,22},{7,23},{8,24},{9,... | collective-permute-start | bytes 1720328 | tf_op jit(solution)/shard_map/ppermute | solution.py:29
  329.0 13.7 %copy-start.8 = (f32[2560]{0:T(1024)S(1)}, f32[2560]{0:T(1024)}, u32[]{:S(2)}) copy-start(f32[2560]{0:T(1024)} %param.19) | copy-start | bytes 30724
  329.0 13.8 %copy-start.9 = (f32[2560]{0:T(1024)S(1)}, f32[2560]{0:T(1024)}, u32[]{:S(2)}) copy-start(f32[2560]{0:T(1024)} %param.20) | copy-start | bytes 30724
  339.2 12.8 %all-to-all-start = ((bf16[4,2,35840]{2,1,0:T(2,128)(2,1)}), bf16[4,2,35840]{2,1,0:T(2,128)(2,1)S(1)}, u32[]{:S(2)}, u32[]{:S(2)}) async-start(bf16[4,2,35840]{2,1,0:T(2,128)(2,1)} %reshape.67), calls=%async_computation | async-start | bytes 1146880 | tf_op jit(solution)/shard_map/all_to_all | solution.py:118
  342.6 401.1 %all-reduce.3.cloned.1.call-start = ((), (), s32[]{:S(2)}) async-start(), calls=%async_computation.3 | async-start | bytes 4587520
  663.7 1.4 copy-start
  663.7 1.4 copy-start.12
  663.8 80.0 %copy-start.7 = (bf16[2,4,14,2560]{3,1,2,0:T(4,128)(2,1)S(1)}, bf16[2,4,14,2560]{3,1,2,0:T(4,128)(2,1)}, u32[]{:S(2)}) copy-start(bf16[2,4,14,2560]{3,1,2,0:T(4,128)(2,1)} %copy-done.6) | copy-start | bytes 1720324
Sparse Core Ops, SparseCore 0:
  8.9 98.3 all-gather.2
  108.8 554.3 all-gather.4
  665.7 78.0 all-reduce.2
